TPU v7x, 32 devices: a whole 2x2x4 slice. The times are simulated.
32 devices in a mesh: grp: 2 (over y), chan: 4 (over z), sub: 4 (over x, core).
Axes of the slice: x: 2, y: 2, z: 4, core: 2. Of those that a mesh axis runs over, the one named last changes fastest.
Arguments:
- voltages: bfloat16 [2048, 2, 5504], P(('grp', 'chan', 'sub')), parts along dimension 0, may hold values from -6 to 6
- taps: float32 [1536], replicated, may hold values from -0.15625 to 0.15625
- input_id: int32 [1024], replicated, may hold values from 0 to 1023, each once
- counts: int32 [8], P('grp'), parts along dimension 0, may hold values from 2 to 8, as said below
- delays: int32 [512, 1024], P(('grp', 'sub')), parts along dimension 0, may hold values from 0 to 127
- beam_owner: int32 [512, 1], P('grp'), parts along dimension 0, may hold values from 0 to 3; in each aligned block of 64 rows (0 to 63, 64 to 127, ...) at most 32 rows name the same one
Outputs:
- visibility: bfloat16 [256, 2, 1024, 1024], P(('grp', 'chan'), None, 'sub'), parts along dimension 0
- resynth: float32 [1024, 2, 5504], P(('grp', 'chan', 'sub')), parts along dimension 0
There are 2 independent parts, one for each index of `grp`. A program takes and returns all parts, laid end to end along the dimension named above; an argument that names none is the same for every part. Nothing has to cross between parts.
Inputs may be any that keep to these rules, and one draw needn't show every extreme that they name: `input_id`: each input id appears once. `counts`: every draw has a block with all 8 spectra valid. `beam_owner`: within each section of 64 consecutive beams no owner is named more than 32 times; some owner is named exactly 32 times in some section.
All inputs are finite; a program needn't handle non-finite values.
Results may differ from a plain program's by a relative error of at most 0.007.
Values may be sent and summed in bfloat16 or wider, within the bound.
A program may use at most 192 MiB of HBM per device.

v0:
```python
import math
import jax
import jax.numpy as jnp
from jax import lax
from jax.sharding import PartitionSpec as P

NCH = 128
TAPS = 12
SPEC = 8
BLOCKS = 4
BEAMS = 256


def filter_table(taps, chans):
    length = taps.shape[0]
    position = jnp.arange(length, dtype=jnp.int32) % chans
    channel = jnp.arange(chans, dtype=jnp.int32)
    phase = (position[:, None] * channel[None, :] % chans).astype(jnp.float32) * (
        2.0 * math.pi / chans
    )
    cosine = taps[:, None] * jnp.cos(phase)
    sine = taps[:, None] * jnp.sin(phase)
    upper = jnp.concatenate([cosine, -sine], axis=1)
    lower = jnp.concatenate([sine, cosine], axis=1)
    return jnp.concatenate([upper, lower], axis=0).astype(jnp.bfloat16)


def resynthesize(received, table, taps_count, chans):
    count = received.shape[0]
    spectra_n = received.shape[3]
    table3 = table.reshape(2 * taps_count * chans, 2, chans)
    grid = jnp.einsum("pcht,mch->ptm", received, table3, preferred_element_type=jnp.float32)
    grid = grid.reshape(count, spectra_n, 2, taps_count, chans)
    total = jnp.zeros((count, spectra_n + taps_count - 1, 2, chans), jnp.float32)
    for k in range(taps_count):
        total = total + jnp.pad(
            grid[:, :, :, k, :], ((0, 0), (k, taps_count - 1 - k), (0, 0), (0, 0))
        )
    return jnp.transpose(total, (0, 2, 1, 3)).reshape(
        count, 2, (spectra_n + taps_count - 1) * chans
    )


def local(voltages, taps, input_id, counts, delays, beam_owner):
    n_chan = lax.axis_size("chan")
    n_sub = lax.axis_size("sub")
    inp_dev = voltages.shape[0]
    inputs = input_id.shape[0]
    chans = NCH
    taps_count = TAPS
    spectra_n = BLOCKS * SPEC
    ch_dev = chans // n_chan
    rows = inputs // n_sub
    section = BEAMS // n_sub
    most = min(section, max(2, 2 * section // n_chan))
    table = filter_table(taps, chans)
    position = jnp.arange(spectra_n, dtype=jnp.int32)
    valid = (position % SPEC < jnp.repeat(counts, SPEC)).astype(jnp.float32)
    total = jnp.sum(counts.astype(jnp.float32))
    frames = voltages.reshape(inp_dev, 2, spectra_n + taps_count - 1, chans)
    windows = jnp.concatenate(
        [frames[:, :, k : k + spectra_n, :] for k in range(taps_count)], axis=3
    )
    table3 = table.reshape(2, taps_count * chans, 2 * chans)
    filtered = jnp.einsum("icth,chm->mit", windows, table3, preferred_element_type=jnp.float32)
    filtered = filtered * valid[None, None, :]
    spectra = filtered.reshape(2, chans, inp_dev, spectra_n).astype(jnp.bfloat16)
    slot_of = jnp.zeros((inputs,), jnp.int32).at[input_id].set(jnp.arange(inputs, dtype=jnp.int32))
    turned = lax.all_to_all(spectra, "chan", split_axis=1, concat_axis=2, tiled=True)
    gathered = lax.all_gather(turned, "sub", axis=2, tiled=True)
    chan_part = slot_of // (n_sub * inp_dev)
    sub_part = slot_of // inp_dev % n_sub
    order = (sub_part * n_chan + chan_part) * inp_dev + slot_of % inp_dev
    by_id = jnp.take(gathered, order, axis=2)
    sub_index = lax.axis_index("sub")
    mine = lax.dynamic_slice_in_dim(by_id, sub_index * rows, rows, 2)
    real_part = jnp.einsum("cxit,cxjt->xij", mine, by_id, preferred_element_type=jnp.float32)
    imag_part = jnp.einsum("xit,xjt->xij", mine[1], by_id[0], preferred_element_type=jnp.float32)
    imag_part = imag_part - jnp.einsum(
        "xit,xjt->xij", mine[0], by_id[1], preferred_element_type=jnp.float32
    )
    visibility = (jnp.stack([real_part, imag_part], axis=1) / total).astype(jnp.bfloat16)
    channel = lax.axis_index("chan") * ch_dev + jnp.arange(ch_dev, dtype=jnp.int32)
    phase = (delays[None, :, :] * channel[:, None, None] % chans).astype(jnp.float32) * (
        2.0 * math.pi / chans
    )
    scale = 1.0 / math.sqrt(inputs)
    weight_cos = (jnp.cos(phase) * scale).astype(jnp.bfloat16)
    weight_sin = (jnp.sin(phase) * scale).astype(jnp.bfloat16)
    from_cos = jnp.einsum("xbi,cxit->cxbt", weight_cos, by_id, preferred_element_type=jnp.float32)
    from_sin = jnp.einsum("xbi,cxit->cxbt", weight_sin, by_id, preferred_element_type=jnp.float32)
    beams = jnp.stack([from_cos[0] - from_sin[1], from_cos[1] + from_sin[0]]).astype(jnp.bfloat16)
    owner = lax.dynamic_slice_in_dim(beam_owner[:, 0], sub_index * section, section)
    beam = jnp.arange(section, dtype=jnp.int32)
    earlier = (owner[None, :] == owner[:, None]) & (beam[None, :] < beam[:, None])
    rank = jnp.sum(earlier.astype(jnp.int32), axis=1)
    target = owner * most + rank
    select = (jnp.arange(n_chan * most, dtype=jnp.int32)[:, None] == target[None, :]).astype(
        jnp.bfloat16
    )
    placed = jnp.einsum("pb,cxbt->pcxt", select, beams, preferred_element_type=jnp.float32).astype(
        jnp.bfloat16
    )
    placed = placed.reshape(n_chan, most, 2, ch_dev, spectra_n)
    resynth = resynthesize(
        lax.all_to_all(placed, "chan", split_axis=0, concat_axis=3, tiled=True)[0],
        table,
        taps_count,
        chans,
    )
    return (visibility, resynth)


def solution(mesh):
    placed = (
        P(("grp", "chan", "sub"), None, None),
        P(),
        P(),
        P("grp"),
        P(("grp", "sub"), None),
        P("grp", None),
    )
    return jax.shard_map(
        local,
        mesh=mesh,
        in_specs=placed,
        out_specs=(P(("grp", "chan"), None, "sub", None), P(("grp", "chan", "sub"), None, None)),
        check_vma=False,
    )
```

profile of v0, /device:TPU:0, one launch (start us, length us, event | category | flops | bytes accessed | tf_op | source)
XLA Modules:
  0.0 464.1 jit_solution(4813590015660750824)
XLA Ops:
  8.0 3.7 reshape.232
  16.0 4.7 %negate_convert_fusion.1 = (bf16[1536,128]{1,0:T(8,128)(2,1)S(1)}, bf16[1536,128]{1,0:T(8,128)(2,1)S(1)}, bf16[1536,128]{1,0:T(8,128)(2,1)S(1)}) fusion(s32[1536]{0:T(1024)S(1)} %add_select_fusion.3, f32[1536]{0:T(1024)S(1)} %copy-done.4), kind=kLoop, calls=%fused_computation.79 | loop fusion | flops 3932160 | bytes 1191936 | tf_op jit(solution)/shard_map/convert.13
  30.2 4.8 %copy-done.3 = bf16[64,2,32,1536]{3,0,1,2:T(8,128)(2,1)} copy-done((bf16[64,2,32,1536]{3,0,1,2:T(8,128)(2,1)}, bf16[64,2,32,1536]{3,0,1,2:T(8,128)(2,1)S(1)}, u32[]{:S(2)}) %copy-start.3) | copy-done | bytes 12582936
  35.1 8.2 %fusion.15 = bf16[256,64,32]{0,1,2:T(8,128)(2,1)S(1)} fusion(bf16[2,1536,256,1]{2,1,0,3:T(8,128)(2,1)S(1)} %bitcast.153, bf16[64,2,32,1536]{3,0,1,2:T(8,128)(2,1)} %copy-done.3, f32[32]{0:T(128)S(1)} %compare_convert_fusion), kind=kOutput, calls=%fused_computation.28 | convolution fusion | flops 3222274048 | bytes 15204480 | tf_op jit(solution)/shard_map/icth,chm->mit/dot_general | solution.py:65
  47.5 32.0 %all_to_all.33 = bf16[4,2,65536]{2,1,0:T(2,128)(2,1)} all-to-all(bf16[4,2,65536]{2,1,0:T(2,128)(2,1)S(1)} %reshape.237), channel_id=1, replica_groups=mesh['grp'=2,'chan'=4,'sub'=4] {'chan'}, dimensions={0} | all-to-all | bytes 2097152 | tf_op jit(solution)/shard_map/all_to_all | solution.py:69
  82.6 6.5 %copy.149 = bf16[2,32,4,64,32]{4,1,3,2,0:T(8,128)(2,1)} copy(bf16[2,32,4,64,32]{3,4,0,1,2:T(8,128)(2,1)S(1)} %bitcast.149) | data formatting | bytes 2097152 | tf_op jit(solution)/shard_map/all_to_all | solution.py:69
  89.2 4.3 scatter_custom_fusion
  94.5 4.2 negate_convert_fusion
  99.9 94.3 %all-gather.2.cloned.1.call-done = bf16[2,32,1024,32]{3,1,2,0:T(8,128)(2,1)} async-done(((bf16[2,32,256,32]{3,1,2,0:T(8,128)(2,1)}), bf16[2,32,1024,32]{3,1,2,0:T(8,128)(2,1)}) %all-gather.2.cloned.1.call-update) | async-done | bytes 4194320 | tf_op jit(solution)/shard_map/all_gather | solution.py:70
  194.3 19.1 %gather_fusion = bf16[1024,2,32,32]{3,2,1,0:T(8,128)(2,1)} fusion(bf16[2,32,1024,32]{3,1,2,0:T(8,128)(2,1)} %all-gather.2.cloned.1.call-done, s32[1024]{0:T(1024)S(1)} %broadcast_clamp_fusion), kind=kCustom, calls=%fused_computation | custom fusion | bytes 8392704 | tf_op jit(solution)/shard_map/jit(_take)/gather | solution.py:74
  213.4 17.5 %copy.109 = bf16[1024,2,32,32]{0,3,1,2:T(8,128)(2,1)} copy(bf16[1024,2,32,32]{3,2,1,0:T(8,128)(2,1)} %gather_fusion) | data formatting | bytes 8388608 | tf_op jit(solution)/shard_map/jit(_take)/gather | solution.py:74
  237.0 31.8 %fusion.21 = f32[2,32,64,32]{2,3,0,1:T(8,128)S(1)} fusion(s32[32]{0:T(128)S(1)} %iota_add_fusion, s32[64,1024]{1,0:T(8,128)S(1)} %copy-done.8, bf16[1024,2,32,32]{0,3,1,2:T(8,128)(2,1)S(1)} %broadcast_select_fusion), kind=kOutput, calls=%fused_computation.35 | convolution fusion | flops 301989888 | bytes 4980864 | tf_op jit(solution)/shard_map/xbi,cxit->cxbt/dot_general | solution.py:90
  268.8 32.1 %fusion.18 = f32[2,32,64,32]{2,3,0,1:T(8,128)S(1)} fusion(s32[32]{0:T(128)S(1)} %iota_add_fusion, s32[64,1024]{1,0:T(8,128)S(1)} %copy-done.8, bf16[1024,2,32,32]{0,3,1,2:T(8,128)(2,1)S(1)} %broadcast_select_fusion), kind=kOutput, calls=%fused_computation.34 | convolution fusion | flops 301989888 | bytes 4980864 | tf_op jit(solution)/shard_map/xbi,cxit->cxbt/dot_general | solution.py:91
  307.3 4.5 reshape.239
  311.8 4.6 all-to-all-start.1
  316.4 15.5 %convolution_bitcast_fusion = f32[32,1,256,1024]{3,2,0,1:T(8,128)} fusion(bf16[2,32,256,32]{2,3,0,1:T(8,128)(2,1)S(1)} %dynamic-slice_bitcast_fusion, bf16[1024,2,32,32]{0,3,1,2:T(8,128)(2,1)} %copy-done.1), kind=kOutput, calls=%fused_computation.8 | convolution fusion | flops 1073741824 | bytes 38797312 | tf_op jit(solution)/shard_map/cxit,cxjt->xij/dot_general | solution.py:77
  331.8 14.0 %fusion.14 = f32[32,256,1024]{2,1,0:T(8,128)} fusion(bf16[2,32,1024,32]{2,3,0,1:T(8,128)(2,1)S(1)} %copy-done.2, bf16[2,32,256,32]{2,3,0,1:T(8,128)(2,1)S(1)} %dynamic-slice_bitcast_fusion), kind=kOutput, calls=%fused_computation.26 | convolution fusion | flops 536870912 | bytes 36175872 | tf_op jit(solution)/shard_map/xit,xjt->xij/dot_general | solution.py:78
  345.9 21.7 %subtract_bitcast_fusion = f32[32,1,256,1024]{3,2,0,1:T(8,128)} fusion(f32[32,256,1024]{2,1,0:T(8,128)} %fusion.14, bf16[2,32,1024,32]{2,3,0,1:T(8,128)(2,1)S(1)} %copy-done.2, bf16[2,32,256,32]{2,3,0,1:T(8,128)(2,1)S(1)} %dynamic-slice_bitcast_fusion), kind=kOutput, calls=%fused_computation.4 | convolution fusion | flops 545259520 | bytes 69730304 | tf_op jit(solution)/shard_map/xit,xjt->xij/dot_general | solution.py:79
  367.5 33.5 %fusion = bf16[32,2,256,1024]{3,2,0,1:T(8,128)(2,1)} fusion(f32[32,1,256,1024]{3,2,0,1:T(8,128)} %subtract_bitcast_fusion, f32[32,1,256,1024]{3,2,0,1:T(8,128)} %convolution_bitcast_fusion, f32[]{:T(128)} %convert_reduce_fusion.1), kind=kLoop, calls=%fused_computation.3 | loop fusion | flops 50331648 | bytes 100663296 | tf_op jit(solution)/shard_map/convert_element_type | solution.py:82
  401.1 23.2 %copy.126 = bf16[32,2,256,1024]{3,2,1,0:T(8,128)(2,1)} copy(bf16[32,2,256,1024]{3,2,0,1:T(8,128)(2,1)} %fusion) | data formatting | bytes 67108864
  427.2 5.2 %copy.112 = bf16[1,32,2,4,32,32]{4,3,5,2,1,0:T(4,128)(2,1)S(1)} copy(bf16[1,32,2,4,32,32]{1,5,4,2,3,0:T(8,128)(2,1)} %bitcast_bitcast_fusion) | data formatting | bytes 1048576 | tf_op jit(solution)/shard_map/all_to_all | solution.py:106
  433.5 7.4 %convolution_bitcast_fusion.1 = f32[32,32,2,12,128]{4,1,3,2,0:T(8,128)} fusion(bf16[2,12,128,2,128]{4,2,1,0,3:T(8,128)(2,1)} %bitcast.152, bf16[32,2,128,32,1,1]{2,3,1,0,4,5:T(8,128)(2,1)S(1)} %reshape.229), kind=kOutput, calls=%fused_computation.16 | convolution fusion | flops 1610612736 | bytes 14680064 | tf_op jit(solution)/shard_map/pcht,mch->ptm/dot_general | solution.py:32
  440.9 9.1 %slice_bitcast_fusion.15 = (f32[32,32,2,128]{3,1,2,0:T(8,128)S(1)}, f32[32,32,2,128]{3,1,2,0:T(8,128)S(1)}, f32[32,32,2,128]{3,1,2,0:T(8,128)S(1)}, f32[32,32,2,...) fusion(f32[32,32,2,12,128]{4,1,3,2,0:T(8,128)} %convolution_bit, ...), kind=kLoop, calls=%fused_computation.54 | loop fusion | bytes 25165824 | tf_op jit(solution)/shard_map/squeeze | solution.py:37
  450.0 5.0 %add_bitcast_fusion = f32[32,2,43,128]{3,2,1,0:T(8,128)S(1)} fusion(f32[32,32,2,128]{3,1,2,0:T(8,128)} %get-tuple-element.22, f32[32,32,2,128]{3,1,2,0:T(8,128)} %get-tuple-element.23, f32[32,32,2,128]{3,1,2,0:T(8,128)S(1)} %get-tuple-element.13, f32[32,32,2,128]{3,1,2,0:T(8,128)S(1)} %get-tuple-element.14, f32[32,32,2,128]{3,1,2,0:T(8,128)S(1)} %get-tuple-element.15, ...), kind=kLoop, calls=%fused_computation.33 | loop fusion | flops 3874816 | bytes 13991936 | tf_op jit(solution)/shard_map/transpose | solution.py:39
  (63 shorter events, 42.4 us)
Async XLA Ops:
  7.2 187.1 %all-gather.2.cloned.1.call-start = ((), (), s32[]{:S(2)}) async-start(), calls=%async_computation.2 | async-start | bytes 20971520 | tf_op jit(solution)/shard_map/all_gather | solution.py:70
  11.7 4.2 copy-start.4
  30.2 4.8 %copy-start.3 = (bf16[64,2,32,1536]{3,0,1,2:T(8,128)(2,1)}, bf16[64,2,32,1536]{3,0,1,2:T(8,128)(2,1)S(1)}, u32[]{:S(2)}) copy-start(bf16[64,2,32,1536]{3,0,1,2:T(8,128)(2,1)S(1)} %copy_dynamic-update-slice_fusion) | copy-start | bytes 37748740
  82.6 6.6 %copy-start.5 = (s32[1024]{0:T(1024)S(1)}, s32[1024]{0:T(1024)}, u32[]{:S(2)}) copy-start(s32[1024]{0:T(1024)} %param.8) | copy-start | bytes 12292
  82.6 10.9 %copy-start.7 = (s32[256,1]{0,1:T(1,128)S(1)}, s32[256,1]{0,1:T(1,128)}, u32[]{:S(2)}) copy-start(s32[256,1]{0,1:T(1,128)} %param.11) | copy-start | bytes 3076
  82.6 11.0 %copy-start.6 = (s32[4]{0:T(128)S(1)}, s32[4]{0:T(128)}, u32[]{:S(2)}) copy-start(s32[4]{0:T(128)} %param.9) | copy-start | bytes 52
  230.9 3.4 copy-start
  234.4 66.6 %copy-start.1 = (bf16[1024,2,32,32]{0,3,1,2:T(8,128)(2,1)}, bf16[1024,2,32,32]{0,3,1,2:T(8,128)(2,1)S(1)}, u32[]{:S(2)}) copy-start(bf16[1024,2,32,32]{0,3,1,2:T(8,128)(2,1)S(1)} %broadcast_select_fusion) | copy-start | bytes 12582916
  234.4 2.7 copy-start.8
  311.8 112.5 %all-to-all-start.1 = ((bf16[4,2,32768]{2,1,0:T(2,128)(2,1)}), bf16[4,2,32768]{2,1,0:T(2,128)(2,1)S(1)}, u32[]{:S(2)}, u32[]{:S(2)}) async-start(bf16[4,2,32768]{2,1,0:T(2,128)(2,1)} %reshape.239), calls=%async_computation.1 | async-start | bytes 1048576 | tf_op jit(solution)/shard_map/all_to_all | solution.py:106
  316.4 15.5 %copy-start.2 = (bf16[2,32,1024,32]{2,3,0,1:T(8,128)(2,1)S(1)}, bf16[2,32,1024,32]{2,3,0,1:T(8,128)(2,1)}, u32[]{:S(2)}) copy-start(bf16[2,32,1024,32]{2,3,0,1:T(8,128)(2,1)} %fusion.78) | copy-start | bytes 12582916
Sparse Core Ops, SparseCore 0:
  89.2 104.9 all-gather.1
where the time goes:
time: 469 us; the launch traced here: 464 us
  matrix products  132 us (28%)
  local copies, waits for them, and re-layouts  131 us (28%)
  waiting for transfers between devices  94.4 us (20%)
  other arithmetic  55.3 us (12%)
  blocking collectives  32 us (7%)
  between operations  14.9 us (3%)
    all_gather x1, waiting for transfers between devices, local(): gathered = lax.all_gather(turned, 'sub', axis=2, tiled=True)  94.3 us
    unnamed x34, local copies, waits for them, and re-layouts  48.3 us
    gather x2, local copies, waits for them, and re-layouts, local(): by_id = jnp.take(gathered, order, axis=2)  36.6 us
    convert_element_type x1, other arithmetic, local(): (jnp.stack([real_part, imag_part], axis=1) / total).astype(jnp.bfloat16)  33.5 us
    dot_general x1, matrix products, local(): jnp.einsum('xbi,cxit->cxbt', weight_sin, by_id, preferred_element_type=jn...  32.1 us
    all_to_all x1, blocking collectives, local(): lax.all_to_all(spectra, 'chan', split_axis=1, concat_axis=2, tiled=True)  32 us
    dot_general x1, matrix products, local(): jnp.einsum('xbi,cxit->cxbt', weight_cos, by_id, preferred_element_type=jn...  31.8 us
    dot_general x1, matrix products, local(): jnp.einsum('xit,xjt->xij', mine[0], by_id[1], preferred_element_type=jnp....  21.7 us
  transfers between devices with their start and end apart: 2, of which 1 were waited for; matrix products, arithmetic and copies ran while one was open for 26% of the time, Pallas kernels for 0%

commit v1 on v0

--- a/solution.py
+++ b/solution.py
@@ -42,6 +42,14 @@
 
 
 def local(voltages, taps, input_id, counts, delays, beam_owner):
+
+    def note_the_routes_all(axis_k, xin):
+        t1 = lax.axis_size("sub")
+        b_next = jnp.concatenate(
+            lax.all_to_all(jnp.stack(t1 * [xin], axis=0), "sub", 0, 0), axis=axis_k
+        )
+        return b_next
+
     n_chan = lax.axis_size("chan")
     n_sub = lax.axis_size("sub")
     inp_dev = voltages.shape[0]
@@ -67,7 +75,7 @@
     spectra = filtered.reshape(2, chans, inp_dev, spectra_n).astype(jnp.bfloat16)
     slot_of = jnp.zeros((inputs,), jnp.int32).at[input_id].set(jnp.arange(inputs, dtype=jnp.int32))
     turned = lax.all_to_all(spectra, "chan", split_axis=1, concat_axis=2, tiled=True)
-    gathered = lax.all_gather(turned, "sub", axis=2, tiled=True)
+    gathered = note_the_routes_all(2, turned)
     chan_part = slot_of // (n_sub * inp_dev)
     sub_part = slot_of // inp_dev % n_sub
     order = (sub_part * n_chan + chan_part) * inp_dev + slot_of % inp_dev

time: 469 us -> 429 us (0.915)
  waiting for transfers between devices: 94.4 us -> 37.4 us
  local copies, waits for them, and re-layouts: 131 us -> 158 us
  between operations: 14.9 us -> 1.47 us
    all_gather x1 -> x0, waiting for transfers between devices: 94.3 us -> none  [local(): gathered = lax.all_gather(turned, 'sub', axis=2, tiled=True)]
    all_to_all x0 -> x1, waiting for transfers between devices: none -> 37.4 us  [note_the_routes_all(): lax.all_to_all(jnp.stack(t1 * [xin], axis=0), 'sub', 0, 0)]
    reshape x0 -> x1, local copies, waits for them, and re-layouts: none -> 23.1 us  [note_the_routes_all(): jnp.concatenate(lax.all_to_all(jnp.stack(t1 * [xin], axis=0), 'sub', 0, 0...]
    another operation x0 -> x2, local copies, waits for them, and re-layouts: none -> 6.04 us  [note_the_routes_all(): jnp.stack(t1 * [xin], axis=0)]
    all_to_all x0 -> x1, starting transfers between devices: none -> 4.97 us  [note_the_routes_all(): lax.all_to_all(jnp.stack(t1 * [xin], axis=0), 'sub', 0, 0)]
  transfers between devices with their start and end apart: 2 -> 2, of which waited for: 1 -> 1; matrix products, arithmetic and copies ran while one was open for 26% -> 28% of each run, Pallas kernels for 0% -> 0%
where the time goes in v1:
time: 429 us; the launch traced here: 424 us
  local copies, waits for them, and re-layouts  158 us (37%)
  matrix products  132 us (31%)
  other arithmetic  55.4 us (13%)
  waiting for transfers between devices  37.4 us (9%)
  blocking collectives  32 us (7%)
  starting transfers between devices  8.44 us (2%)
    unnamed x34, local copies, waits for them, and re-layouts  48.3 us
    all_to_all x1, waiting for transfers between devices, note_the_routes_all(): lax.all_to_all(jnp.stack(t1 * [xin], axis=0), 'sub', 0, 0)  37.4 us
    gather x2, local copies, waits for them, and re-layouts, local(): by_id = jnp.take(gathered, order, axis=2)  36.7 us
    convert_element_type x1, other arithmetic, local(): (jnp.stack([real_part, imag_part], axis=1) / total).astype(jnp.bfloat16)  33.5 us
    dot_general x1, matrix products, local(): jnp.einsum('xbi,cxit->cxbt', weight_sin, by_id, preferred_element_type=jn...  32.1 us
    all_to_all x1, blocking collectives, local(): lax.all_to_all(spectra, 'chan', split_axis=1, concat_axis=2, tiled=True)  32 us
    dot_general x1, matrix products, local(): jnp.einsum('xbi,cxit->cxbt', weight_cos, by_id, preferred_element_type=jn...  31.8 us
    reshape x1, local copies, waits for them, and re-layouts, note_the_routes_all(): jnp.concatenate(lax.all_to_all(jnp.stack(t1 * [xin], axis=0), 'sub', 0, 0...  23.1 us
  transfers between devices with their start and end apart: 2, of which 1 were waited for; matrix products, arithmetic and copies ran while one was open for 28% of the time, Pallas kernels for 0%

profile of v1, /device:TPU:0, one launch (start us, length us, event | category | flops | bytes accessed | tf_op | source)
XLA Modules:
  0.0 424.2 jit_solution(11493541644977457212)
XLA Ops:
  9.4 4.7 %negate_convert_fusion.1 = (bf16[1536,128]{1,0:T(8,128)(2,1)S(1)}, bf16[1536,128]{1,0:T(8,128)(2,1)S(1)}, bf16[1536,128]{1,0:T(8,128)(2,1)S(1)}) fusion(s32[1536]{0:T(1024)S(1)} %add_select_fusion.3, f32[1536]{0:T(1024)S(1)} %copy-done.4), kind=kLoop, calls=%fused_computation.79 | loop fusion | flops 3932160 | bytes 1191936 | tf_op jit(solution)/shard_map/convert.13
  23.6 4.8 %copy-done.3 = bf16[64,2,32,1536]{3,0,1,2:T(8,128)(2,1)} copy-done((bf16[64,2,32,1536]{3,0,1,2:T(8,128)(2,1)}, bf16[64,2,32,1536]{3,0,1,2:T(8,128)(2,1)S(1)}, u32[]{:S(2)}) %copy-start.3) | copy-done | bytes 12582936
  28.5 8.3 %fusion.15 = bf16[256,64,32]{0,1,2:T(8,128)(2,1)S(1)} fusion(bf16[2,1536,256,1]{2,1,0,3:T(8,128)(2,1)S(1)} %bitcast.156, bf16[64,2,32,1536]{3,0,1,2:T(8,128)(2,1)} %copy-done.3, f32[32]{0:T(128)S(1)} %compare_convert_fusion), kind=kOutput, calls=%fused_computation.28 | convolution fusion | flops 3222274048 | bytes 15204480 | tf_op jit(solution)/shard_map/icth,chm->mit/dot_general | solution.py:73
  40.9 32.0 %all_to_all.35 = bf16[4,2,65536]{2,1,0:T(2,128)(2,1)} all-to-all(bf16[4,2,65536]{2,1,0:T(2,128)(2,1)S(1)} %reshape.248), channel_id=1, replica_groups=mesh['grp'=2,'chan'=4,'sub'=4] {'chan'}, dimensions={0} | all-to-all | bytes 2097152 | tf_op jit(solution)/shard_map/all_to_all | solution.py:77
  76.0 4.0 copy.108
  86.1 5.0 %all-to-all-start.1 = ((bf16[4,2,32,256,32]{3,4,2,1,0:T(8,128)(2,1)}), bf16[4,2,32,256,32]{3,4,2,1,0:T(8,128)(2,1)}, u32[]{:S(2)}, u32[]{:S(2)}) async-start(bf16[4,2,32,256,32]{3,4,2,1,0:T(8,128)(2,1)} %stack.25), calls=%async_computation.1 | async-start | bytes 8388608 | tf_op jit(solution)/shard_map/all_to_all | solution.py:49
  91.1 4.3 %scatter_custom_fusion = s32[1024]{0:T(1024)S(1)} fusion(s32[1024]{0:T(1024)S(1)} %compare_select_fusion.1, s32[1024]{0:T(1024)S(1)} %iota.42, s32[]{:T(128)} %constant.113.clone.1), kind=kCustom, calls=%fused_computation.134 | custom fusion | bytes 4100 | tf_op jit(solution)/shard_map/scatter | solution.py:76
  96.4 4.2 negate_convert_fusion
  101.9 37.4 %all-to-all-done.1 = bf16[4,2,32,256,32]{3,4,2,1,0:T(8,128)(2,1)} async-done(((bf16[4,2,32,256,32]{3,4,2,1,0:T(8,128)(2,1)}), bf16[4,2,32,256,32]{3,4,2,1,0:T(8,128)(2,1)}, u32[]{:S(2)}, u32[]{:S(2)}) %all-to-all-start.1) | async-done | bytes 4194336 | tf_op jit(solution)/shard_map/all_to_all | solution.py:49
  139.3 23.1 %copy.151 = bf16[2,32,4,256,32]{4,1,3,2,0:T(8,128)(2,1)} copy(bf16[2,32,4,256,32]{3,4,1,0,2:T(8,128)(2,1)} %bitcast.7) | data formatting | bytes 8388608 | tf_op jit(solution)/shard_map/reshape | solution.py:48
  162.3 19.2 %gather_fusion = bf16[1024,2,32,32]{3,2,1,0:T(8,128)(2,1)} fusion(bf16[2,32,1024,32]{3,1,2,0:T(8,128)(2,1)} %bitcast.151, s32[1024]{0:T(1024)S(1)} %broadcast_clamp_fusion), kind=kCustom, calls=%fused_computation | custom fusion | bytes 8392704 | tf_op jit(solution)/shard_map/jit(_take)/gather | solution.py:82
  181.5 17.5 %copy.111 = bf16[1024,2,32,32]{0,3,1,2:T(8,128)(2,1)} copy(bf16[1024,2,32,32]{3,2,1,0:T(8,128)(2,1)} %gather_fusion) | data formatting | bytes 8388608 | tf_op jit(solution)/shard_map/jit(_take)/gather | solution.py:82
  205.1 31.8 %fusion.21 = f32[2,32,64,32]{2,3,0,1:T(8,128)S(1)} fusion(s32[32]{0:T(128)S(1)} %iota_add_fusion, s32[64,1024]{1,0:T(8,128)S(1)} %copy-done.8, bf16[1024,2,32,32]{0,3,1,2:T(8,128)(2,1)S(1)} %broadcast_select_fusion), kind=kOutput, calls=%fused_computation.35 | convolution fusion | flops 301989888 | bytes 4980864 | tf_op jit(solution)/shard_map/xbi,cxit->cxbt/dot_general | solution.py:98
  236.9 32.1 %fusion.18 = f32[2,32,64,32]{2,3,0,1:T(8,128)S(1)} fusion(s32[32]{0:T(128)S(1)} %iota_add_fusion, s32[64,1024]{1,0:T(8,128)S(1)} %copy-done.8, bf16[1024,2,32,32]{0,3,1,2:T(8,128)(2,1)S(1)} %broadcast_select_fusion), kind=kOutput, calls=%fused_computation.34 | convolution fusion | flops 301989888 | bytes 4980864 | tf_op jit(solution)/shard_map/xbi,cxit->cxbt/dot_general | solution.py:99
  275.4 4.5 %reshape.250 = bf16[4,2,32768]{2,1,0:T(2,128)(2,1)} reshape(bf16[4,2,32,32,32]{4,3,2,1,0:T(8,128)(2,1)} %bitcast.153) | data formatting | bytes 1048576
  283.3 15.5 %convolution_bitcast_fusion = f32[32,1,256,1024]{3,2,0,1:T(8,128)} fusion(bf16[2,32,256,32]{2,3,0,1:T(8,128)(2,1)S(1)} %dynamic-slice_bitcast_fusion, bf16[1024,2,32,32]{0,3,1,2:T(8,128)(2,1)} %copy-done.1), kind=kOutput, calls=%fused_computation.8 | convolution fusion | flops 1073741824 | bytes 38797312 | tf_op jit(solution)/shard_map/cxit,cxjt->xij/dot_general | solution.py:85
  298.8 14.0 %fusion.14 = f32[32,256,1024]{2,1,0:T(8,128)} fusion(bf16[2,32,1024,32]{2,3,0,1:T(8,128)(2,1)S(1)} %copy-done.2, bf16[2,32,256,32]{2,3,0,1:T(8,128)(2,1)S(1)} %dynamic-slice_bitcast_fusion), kind=kOutput, calls=%fused_computation.26 | convolution fusion | flops 536870912 | bytes 36175872 | tf_op jit(solution)/shard_map/xit,xjt->xij/dot_general | solution.py:86
  312.9 21.7 %subtract_bitcast_fusion = f32[32,1,256,1024]{3,2,0,1:T(8,128)} fusion(f32[32,256,1024]{2,1,0:T(8,128)} %fusion.14, bf16[2,32,1024,32]{2,3,0,1:T(8,128)(2,1)S(1)} %copy-done.2, bf16[2,32,256,32]{2,3,0,1:T(8,128)(2,1)S(1)} %dynamic-slice_bitcast_fusion), kind=kOutput, calls=%fused_computation.4 | convolution fusion | flops 545259520 | bytes 69730304 | tf_op jit(solution)/shard_map/xit,xjt->xij/dot_general | solution.py:87
  334.5 33.5 %fusion = bf16[32,2,256,1024]{3,2,0,1:T(8,128)(2,1)} fusion(f32[32,1,256,1024]{3,2,0,1:T(8,128)} %subtract_bitcast_fusion, f32[32,1,256,1024]{3,2,0,1:T(8,128)} %convolution_bitcast_fusion, f32[]{:T(128)} %convert_reduce_fusion.1), kind=kLoop, calls=%fused_computation.3 | loop fusion | flops 50331648 | bytes 100663296 | tf_op jit(solution)/shard_map/convert_element_type | solution.py:90
  368.1 23.2 %copy.128 = bf16[32,2,256,1024]{3,2,1,0:T(8,128)(2,1)} copy(bf16[32,2,256,1024]{3,2,0,1:T(8,128)(2,1)} %fusion) | data formatting | bytes 67108864
  394.2 5.2 %copy.114 = bf16[1,32,2,4,32,32]{4,3,5,2,1,0:T(4,128)(2,1)S(1)} copy(bf16[1,32,2,4,32,32]{1,5,4,2,3,0:T(8,128)(2,1)} %bitcast_bitcast_fusion) | data formatting | bytes 1048576 | tf_op jit(solution)/shard_map/all_to_all | solution.py:114
  400.5 7.4 %convolution_bitcast_fusion.1 = f32[32,32,2,12,128]{4,1,3,2,0:T(8,128)} fusion(bf16[2,12,128,2,128]{4,2,1,0,3:T(8,128)(2,1)} %bitcast.155, bf16[32,2,128,32,1,1]{2,3,1,0,4,5:T(8,128)(2,1)S(1)} %reshape.240), kind=kOutput, calls=%fused_computation.16 | convolution fusion | flops 1610612736 | bytes 14680064 | tf_op jit(solution)/shard_map/pcht,mch->ptm/dot_general | solution.py:32
  407.9 9.1 %slice_bitcast_fusion.15 = (f32[32,32,2,128]{3,1,2,0:T(8,128)S(1)}, f32[32,32,2,128]{3,1,2,0:T(8,128)S(1)}, f32[32,32,2,128]{3,1,2,0:T(8,128)S(1)}, f32[32,32,2,...) fusion(f32[32,32,2,12,128]{4,1,3,2,0:T(8,128)} %convolution_bit, ...), kind=kLoop, calls=%fused_computation.54 | loop fusion | bytes 25165824 | tf_op jit(solution)/shard_map/squeeze | solution.py:37
  417.0 5.0 %add_bitcast_fusion = f32[32,2,43,128]{3,2,1,0:T(8,128)S(1)} fusion(f32[32,32,2,128]{3,1,2,0:T(8,128)} %get-tuple-element.22, f32[32,32,2,128]{3,1,2,0:T(8,128)} %get-tuple-element.23, f32[32,32,2,128]{3,1,2,0:T(8,128)S(1)} %get-tuple-element.13, f32[32,32,2,128]{3,1,2,0:T(8,128)S(1)} %get-tuple-element.14, f32[32,32,2,128]{3,1,2,0:T(8,128)S(1)} %get-tuple-element.15, ...), kind=kLoop, calls=%fused_computation.33 | loop fusion | flops 3874816 | bytes 13991936 | tf_op jit(solution)/shard_map/transpose | solution.py:39
  (65 shorter events, 55.5 us)
Async XLA Ops:
  5.1 4.2 copy-start.4
  23.6 4.8 %copy-start.3 = (bf16[64,2,32,1536]{3,0,1,2:T(8,128)(2,1)}, bf16[64,2,32,1536]{3,0,1,2:T(8,128)(2,1)S(1)}, u32[]{:S(2)}) copy-start(bf16[64,2,32,1536]{3,0,1,2:T(8,128)(2,1)S(1)} %copy_dynamic-update-slice_fusion) | copy-start | bytes 37748740
  86.1 5.0 %copy-start.5 = (s32[1024]{0:T(1024)S(1)}, s32[1024]{0:T(1024)}, u32[]{:S(2)}) copy-start(s32[1024]{0:T(1024)} %param.8) | copy-start | bytes 12292
  86.1 9.4 %copy-start.7 = (s32[256,1]{0,1:T(1,128)S(1)}, s32[256,1]{0,1:T(1,128)}, u32[]{:S(2)}) copy-start(s32[256,1]{0,1:T(1,128)} %param.11) | copy-start | bytes 3076
  86.1 9.4 %copy-start.6 = (s32[4]{0:T(128)S(1)}, s32[4]{0:T(128)}, u32[]{:S(2)}) copy-start(s32[4]{0:T(128)} %param.9) | copy-start | bytes 52
  86.1 53.2 %all-to-all-start.1 = ((bf16[4,2,32,256,32]{3,4,2,1,0:T(8,128)(2,1)}), bf16[4,2,32,256,32]{3,4,2,1,0:T(8,128)(2,1)}, u32[]{:S(2)}, u32[]{:S(2)}) async-start(bf16[4,2,32,256,32]{3,4,2,1,0:T(8,128)(2,1)} %stack.25), calls=%async_computation.1 | async-start | bytes 8388608 | tf_op jit(solution)/shard_map/all_to_all | solution.py:49
  199.0 3.4 copy-start
  202.5 66.6 %copy-start.1 = (bf16[1024,2,32,32]{0,3,1,2:T(8,128)(2,1)}, bf16[1024,2,32,32]{0,3,1,2:T(8,128)(2,1)S(1)}, u32[]{:S(2)}) copy-start(bf16[1024,2,32,32]{0,3,1,2:T(8,128)(2,1)S(1)} %broadcast_select_fusion) | copy-start | bytes 12582916
  202.5 2.7 copy-start.8
  279.9 111.5 %all-to-all-start.2 = ((bf16[4,2,32768]{2,1,0:T(2,128)(2,1)}), bf16[4,2,32768]{2,1,0:T(2,128)(2,1)S(1)}, u32[]{:S(2)}, u32[]{:S(2)}) async-start(bf16[4,2,32768]{2,1,0:T(2,128)(2,1)} %reshape.250), calls=%async_computation.2 | async-start | bytes 1048576 | tf_op jit(solution)/shard_map/all_to_all | solution.py:114
  283.3 15.5 %copy-start.2 = (bf16[2,32,1024,32]{2,3,0,1:T(8,128)(2,1)S(1)}, bf16[2,32,1024,32]{2,3,0,1:T(8,128)(2,1)}, u32[]{:S(2)}) copy-start(bf16[2,32,1024,32]{2,3,0,1:T(8,128)(2,1)} %fusion.78) | copy-start | bytes 12582916
